TPU v7x, 32 devices: a whole 2x2x4 slice. The times are simulated.
32 devices in a mesh: groups: 2 (over x), ctx: 16 (over z, y, core).
Axes of the slice: x: 2, y: 2, z: 4, core: 2. Of those that a mesh axis runs over, the one named last changes fastest.
Arguments:
- queries: bfloat16 [2048, 256], P(('groups', 'ctx')), parts along dimension 0, may hold values from -60 to 60
- keys: bfloat16 [2048, 128], P(('groups', 'ctx')), parts along dimension 0, may hold values from -6 to 6
- values: bfloat16 [2048, 128], P(('groups', 'ctx')), parts along dimension 0, may hold values from -96 to 96
- span_section: int32 [32], P(('groups', 'ctx')), parts along dimension 0, may hold values from 0 to 7, as said below
- query_section: int32 [64], P('groups'), parts along dimension 0, may hold values from 0 to 7, as said below
- section_queries: bfloat16 [64, 256], P('groups'), parts along dimension 0, may hold values from -60 to 60
- out_proj: bfloat16 [256, 4608], replicated, may hold values from -0.375 to 0.375
- norm_gain: bfloat16 [4608], replicated, may hold values from 0.099609375 to 1.8984375
- up_weight: bfloat16 [4608, 4096], P(None, 'ctx'), may hold values from -0.09375 to 0.09375
- down_weight: bfloat16 [4096, 4608], P('ctx'), may hold values from -0.125 to 0.125
Outputs:
- context: bfloat16 [2048, 256], P(('groups', 'ctx')), parts along dimension 0
- section_out: bfloat16 [64, 4608], P('groups', 'ctx'), parts along dimension 0
There are 2 independent parts, one for each index of `groups`. A program takes and returns all parts, laid end to end along the dimension named above; an argument that names none is the same for every part. Nothing has to cross between parts.
Inputs may be any that keep to these rules, and one draw needn't show every extreme that they name: `span_section`: sections are runs of whole spans in order; every section holds one span or more. `query_section`: every section is read by exactly 4 section queries.
All inputs are finite; a program needn't handle non-finite values.
Results may differ from a plain program's by a relative error of at most 0.018.
Values may be sent and summed in bfloat16 or wider, within the bound.
A program may use at most 128 MiB of HBM per device.

v0:
```python
import jax
import jax.numpy as jnp
from jax import lax
from jax.sharding import PartitionSpec as P

HD = 128
HQ = 2
SPAN = 64


def combined_all(array, axis, join):
    gathered = jax.tree.map(
        lambda a, kind: lax.all_gather(a.astype(kind), axis),
        array,
        (jnp.bfloat16, jnp.bfloat16, jnp.bfloat16),
    )

    def take(source):
        return jax.tree.map(
            lambda a, own: lax.dynamic_index_in_dim(a, source, 0, False).astype(own.dtype),
            gathered,
            array,
        )

    return lax.fori_loop(
        1, lax.axis_size(axis), lambda source, state: join(state, take(source)), take(0)
    )


def softmax_join(first, second):
    top = jnp.maximum(first[0], second[0])
    left = jnp.exp(first[0] - top)
    right = jnp.exp(second[0] - top)
    return (
        top,
        first[1] * left + second[1] * right,
        first[2] * left[..., None] + second[2] * right[..., None],
    )


def per_device(
    queries,
    keys,
    values,
    span_section,
    query_section,
    section_queries,
    out_proj,
    norm_gain,
    up_weight,
    down_weight,
):
    scale = HD ** (-0.5)
    rows = queries.shape[0]
    flat = queries.reshape(rows * HQ, HD)
    start_state = (
        jnp.full((rows * HQ,), -1e30, jnp.float32),
        jnp.zeros((rows * HQ,), jnp.float32),
        jnp.zeros((rows * HQ, HD), jnp.float32),
    )
    key_piece = lax.all_gather(keys, "ctx", axis=0, tiled=True)
    value_piece = lax.all_gather(values, "ctx", axis=0, tiled=True)
    count = key_piece.shape[0]
    width = 512

    def one_block(state, index):
        key_block = lax.dynamic_slice_in_dim(key_piece, index * width, width, 0)
        value_block = lax.dynamic_slice_in_dim(value_piece, index * width, width, 0)
        scores = (
            lax.dot_general(
                flat, key_block, (((1,), (1,)), ((), ())), preferred_element_type=jnp.float32
            )
            * scale
        )
        top = jnp.maximum(state[0], jnp.max(scores, axis=1))
        shrink = jnp.exp(state[0] - top)
        weights = jnp.exp(scores - top[:, None])
        total = state[1] * shrink + jnp.sum(weights, axis=1)
        summed = state[2] * shrink[:, None] + jnp.dot(
            weights.astype(jnp.bfloat16), value_block, preferred_element_type=jnp.float32
        )
        return ((top, total, summed), None)

    result, unused = lax.scan(one_block, start_state, jnp.arange(count // width))
    context = (result[2] / result[1][:, None]).reshape(rows, HQ * HD).astype(jnp.bfloat16)
    sections = section_queries.shape[0]
    token_section = jnp.repeat(span_section, SPAN)
    admitted = (query_section[:, None] == token_section[None, :])[:, None, :]
    cross = (
        lax.dot_general(
            section_queries.reshape(sections * HQ, HD),
            keys,
            (((1,), (1,)), ((), ())),
            preferred_element_type=jnp.float32,
        )
        * scale
    )
    cross = cross.reshape(sections, HQ, rows)
    local_top = jnp.max(jnp.where(admitted, cross, jnp.float32(-1e30)), axis=2)
    context_heads = context.reshape(rows, HQ, HD)
    cross_weights = jnp.where(admitted, jnp.exp(cross - local_top[:, :, None]), jnp.float32(0.0))
    local_total = jnp.sum(cross_weights, axis=2)
    local_sum = jnp.einsum(
        "shu,uhd->shd",
        cross_weights.astype(jnp.bfloat16),
        context_heads,
        preferred_element_type=jnp.float32,
    )
    top, cross_total, summed = combined_all(
        (local_top, local_total, local_sum), "ctx", softmax_join
    )
    pooled = (summed / cross_total[:, :, None]).reshape(sections, HQ * HD).astype(jnp.bfloat16)
    embed = jnp.dot(pooled, out_proj, preferred_element_type=jnp.float32)
    normed = (
        embed
        * lax.rsqrt(jnp.mean(embed * embed, axis=1, keepdims=True) + 1e-06)
        * norm_gain.astype(jnp.float32)
    )
    normed = normed.astype(jnp.bfloat16)
    hidden = jax.nn.gelu(jnp.dot(normed, up_weight, preferred_element_type=jnp.float32)).astype(
        jnp.bfloat16
    )
    share = lax.psum_scatter(
        lax.dot_general(
            down_weight, hidden, (((0,), (1,)), ((), ())), preferred_element_type=jnp.float32
        ),
        "ctx",
        scatter_dimension=0,
        tiled=True,
    )
    section_out = share.T.astype(jnp.bfloat16)
    return (context, section_out)


def solution(mesh):
    in_specs = (
        P(("groups", "ctx"), None),
        P(("groups", "ctx"), None),
        P(("groups", "ctx"), None),
        P(("groups", "ctx")),
        P("groups"),
        P("groups", None),
        P(),
        P(),
        P(None, "ctx"),
        P("ctx", None),
    )
    out_specs = (P(("groups", "ctx"), None), P("groups", "ctx"))
    return jax.shard_map(
        per_device, mesh=mesh, in_specs=in_specs, out_specs=out_specs, check_vma=False
    )
```

profile of v0, /device:TPU:0, one launch (start us, length us, event | category | flops | bytes accessed | tf_op | source)
XLA Modules:
  0.0 198.3 jit_solution(2779631945923353458)
XLA Ops:
  8.0 0.7 broadcast_compare_fusion
  8.9 0.7 reshape.90
  9.6 0.9 select_reduce_fusion.1
  10.7 24.1 %all_gather.20 = bf16[1024,128]{1,0:T(8,128)(2,1)S(1)} all-gather(bf16[64,128]{1,0:T(8,128)(2,1)} %param.15), channel_id=1, replica_groups=mesh['groups'=2,'ctx'=16] {'ctx'}, dimensions={0}, use_global_device_ids=true | all-gather | bytes 278528 | tf_op jit(solution)/shard_map/all_gather | solution.py:61
  35.0 17.4 %all_gather.22 = bf16[16,32,2]{1,2,0:T(2,128)(2,1)S(1)} all-gather(bf16[1,32,2]{1,2,0:T(2,128)(2,1)S(1)} %copy.38), channel_id=1, replica_groups=mesh['groups'=2,'ctx'=16] {'ctx'}, dimensions={0}, use_global_device_ids=true | all-gather | bytes 2176 | tf_op jit(solution)/shard_map/all_gather | solution.py:13
  52.7 18.8 %all_gather.23 = bf16[16,32,2]{1,2,0:T(2,128)(2,1)S(1)} all-gather(bf16[1,32,2]{1,2,0:T(2,128)(2,1)S(1)} %copy.39), channel_id=1, replica_groups=mesh['groups'=2,'ctx'=16] {'ctx'}, dimensions={0}, use_global_device_ids=true | all-gather | bytes 2176 | tf_op jit(solution)/shard_map/all_gather | solution.py:13
  71.5 1.3 convert_element_type.145
  72.8 0.8 reshape.89
  73.5 18.4 %all_gather.21 = bf16[1024,128]{1,0:T(8,128)(2,1)S(1)} all-gather(bf16[64,128]{1,0:T(8,128)(2,1)} %param.16), channel_id=1, replica_groups=mesh['groups'=2,'ctx'=16] {'ctx'}, dimensions={0}, use_global_device_ids=true | all-gather | bytes 278528 | tf_op jit(solution)/shard_map/all_gather | solution.py:62
  91.9 3.6 %while.35 = (s32[]{:T(128)}, f32[128]{0:T(128)S(1)}, f32[128]{0:T(128)S(1)}, f32[128,128]{1,0:T(8,128)S(1)}, s32[2]{0:T(128)S(1)}, /*index=5*/bf16[1024,128]{1,0...) while((s32[]{:T(128)}, f32[128]{0:T(128)S(1)}, ...), condition=%wide.region_3.4_spmd.clone, body=%wide.region_0.3_spmd.clone.sunk | while | flops 33997444 | bytes 1220811 | solution.py:84
  91.9 0.6 dynamic_slice.95
  93.1 0.2 fusion.65
  93.5 0.2 convolution_add_fusion.2
  93.7 0.6 dynamic_slice.95
  94.9 0.2 fusion.65
  95.2 0.2 convolution_add_fusion.2
  95.9 19.4 %all-gather = bf16[512,2,128]{2,0,1:T(8,128)(2,1)S(1)} all-gather(bf16[32,2,128]{2,0,1:T(8,128)(2,1)S(1)} %fusion.16), channel_id=2, replica_groups=mesh['groups'=2,'ctx'=16] {'ctx'}, dimensions={0}, use_global_device_ids=true | all-gather | bytes 278528 | tf_op jit(solution)/shard_map/all_gather | solution.py:13
  115.4 7.1 %while.34 = (s32[]{:T(128)}, f32[32,2]{0,1:T(2,128)S(1)}, f32[32,2]{0,1:T(2,128)S(1)}, f32[32,2,128]{2,1,0:T(2,128)S(1)}, bf16[16,32,2]{1,2,0:T(2,128)(2,1)S(1)}...) while((s32[]{:T(128)}, f32[32,2]{0,1:T(2,128)S(1)}, ...), condition=%wide.region_7.8_spmd, body=%wide.region_6.7_spmd.sunk | while | flops 33285 | bytes 118159 | solution.py:25
  115.6 0.2 fusion.61
  116.1 0.2 fusion.61
  116.5 0.2 fusion.61
  117.5 0.2 fusion.61
  118.0 0.2 fusion.61
  118.4 0.2 fusion.61
  118.9 0.2 fusion.61
  119.4 0.2 fusion.61
  122.7 0.6 multiply_reduce_fusion
  123.3 3.9 %convolution_bitcast_fusion = f32[4608,32]{0,1:T(8,128)S(1)} fusion(bf16[256,4608]{1,0:T(8,128)(2,1)} %param.23, bf16[4608,256]{1,0:T(8,128)(2,1)} %param.22, f32[32,4608]{1,0:T(8,128)S(1)} %get-tuple-element.315, f32[4608]{0:T(1024)} %convert_element_type.145, f32[32]{0:T(128)S(1)} %add_rsqrt_fusion), kind=kOutput, calls=%fused_computation.31 | convolution fusion | flops 151511040 | bytes 5916800 | tf_op jit(solution)/shard_map/dot_general | solution.py:124
  127.2 2.1 %copy.46 = f32[4608,32]{1,0:T(8,128)} copy(f32[4608,32]{0,1:T(8,128)S(1)} %convolution_bitcast_fusion) | data formatting | bytes 1179648
  129.3 0.6 convert_element_type.128
  129.9 60.0 %reduce-scatter.4.cloned.1.call-done = f32[288,32]{1,0:T(8,128)} async-done(((f32[4608,32]{1,0:T(8,128)}), f32[288,32]{1,0:T(8,128)}) %reduce-scatter.4.cloned.1.call-update) | async-done | bytes 36880
  189.9 1.6 copy.47
  (107 shorter events, 6.5 us)
Async XLA Ops:
  7.2 115.5 %copy-start = (bf16[256,4608]{1,0:T(8,128)(2,1)S(1)}, bf16[256,4608]{1,0:T(8,128)(2,1)}, u32[]{:S(2)}) copy-start(bf16[256,4608]{1,0:T(8,128)(2,1)} %param.20) | copy-start | bytes 7077892
  7.2 182.7 %reduce-scatter.4.cloned.1.call-start = ((), (), s32[]{:S(2)}) async-start(), calls=%async_computation.1 | async-start | bytes 2506752
  95.8 19.6 %copy-start.1 = (bf16[128,128]{1,0:T(8,128)(2,1)}, bf16[128,128]{1,0:T(8,128)(2,1)S(1)}, u32[]{:S(2)}) copy-start(bf16[128,128]{1,0:T(8,128)(2,1)S(1)} %divide_convert_fusion) | copy-start | bytes 98308
  127.2 2.1 %copy-start.2 = (bf16[128,128]{1,0:T(8,128)(2,1)S(1)}, bf16[128,128]{1,0:T(8,128)(2,1)}, u32[]{:S(2)}) copy-start(bf16[128,128]{1,0:T(8,128)(2,1)} %copy-done.1) | copy-start | bytes 98308
Sparse Core Ops, SparseCore 0:
  129.4 60.4 reduce-scatter.3
where the time goes:
time: 199 us; the launch traced here: 198 us
  blocking collectives  98.1 us (49%)
  waiting for transfers between devices  60 us (30%)
  between operations  15 us (8%)
  local copies, waits for them, and re-layouts  10.6 us (5%)
  other arithmetic  6.53 us (3%)
  matrix products  6.43 us (3%)
    unnamed x2, waiting for transfers between devices  60 us
    all_gather x3, blocking collectives, combined_all(): lax.all_gather(a.astype(kind), axis)  55.7 us
    all_gather x1, blocking collectives, per_device(): key_piece = lax.all_gather(keys, 'ctx', axis=0, tiled=True)  24.1 us
    all_gather x1, blocking collectives, per_device(): value_piece = lax.all_gather(values, 'ctx', axis=0, tiled=True)  18.4 us
  transfers between devices with their start and end apart: 1, of which 1 were waited for; matrix products, arithmetic and copies ran while one was open for 0% of the time, Pallas kernels for 0%

commit v1 on v0

v1 whole, which is shorter than its diff:
```python
import functools

import jax
import jax.numpy as jnp
from jax import lax
from jax.experimental import pallas as pl
from jax.experimental.pallas import tpu as pltpu
from jax.sharding import PartitionSpec as P

HD = 128
HQ = 2
SPAN = 64
READERS = 4
CHUNK = 1024
SLOTS = HQ * READERS

F32 = jnp.float32
BF16 = jnp.bfloat16
MESH = pl.DeviceIdType.MESH


def each(low, high, body):
    if high - low <= 16:
        for k in range(low, high):
            body(k)
    else:
        pl.loop(low, high)(body)


def dims(a, b):
    return (((a,), (b,)), ((), ()))


def dot(a, b, ca=1, cb=0):
    return lax.dot_general(a, b, dims(ca, cb), preferred_element_type=F32)


def iota(shape, axis):
    return lax.broadcasted_iota(jnp.int32, shape, axis)


def kernel(
    n,
    q_ref,
    k_ref,
    v_ref,
    span_ref,
    qsec_ref,
    sq_ref,
    o_ref,
    gain_ref,
    up_ref,
    down_ref,
    ctx_ref,
    out_ref,
    kv,
    sec,
    part,
    gath,
    ov,
    upv,
    downv,
    yb,
    rb,
    sb,
    fb,
    wsem,
    kvsem,
    ag_send,
    ag_recv,
    rl_send,
    rl_recv,
    sc_send,
    sc_recv,
    pt_send,
    pt_recv,
    pr_send,
    pr_recv,
    fn_send,
    fn_recv,
):
    scale = HD ** (-0.5)
    chips = n // 2
    me = lax.axis_index("ctx")
    chip = me // 2
    core = me % 2
    partner = me + 1 - 2 * core
    rows = q_ref.shape[0]
    tokens = n * rows
    count = qsec_ref.shape[1]

    own = kv.at[me]
    kcopy = pltpu.make_async_copy(k_ref, own.at[:, 0:HD], kvsem.at[0])
    vcopy = pltpu.make_async_copy(v_ref, own.at[:, HD : 2 * HD], kvsem.at[1])
    kcopy.start()
    vcopy.start()
    weights = [
        pltpu.make_async_copy(o_ref, ov, wsem.at[0]),
        pltpu.make_async_copy(up_ref, upv, wsem.at[1]),
        pltpu.make_async_copy(down_ref, downv, wsem.at[2]),
    ]
    for w in weights:
        w.start()

    mine = jnp.broadcast_to(span_ref[0, 0], (1, HD))
    sec[me] = mine

    barrier = pltpu.get_barrier_semaphore()

    def greet(k):
        pl.semaphore_signal(
            barrier, inc=1, device_id={"ctx": lax.rem(me + k, n)}, device_id_type=MESH
        )

    each(1, n, greet)
    pl.semaphore_wait(barrier, n - 1)
    kcopy.wait()
    vcopy.wait()

    def remote(src, dst, send, recv, to):
        return pltpu.make_async_remote_copy(
            src_ref=src,
            dst_ref=dst,
            send_sem=send,
            recv_sem=recv,
            device_id={"ctx": to},
            device_id_type=MESH,
        )

    def gather_copy(k):
        to = lax.rem(chip + k, chips) * 2 + core
        return remote(own, own, ag_send.at[k - 1], ag_recv.at[k - 1], to)

    def arrived_block(k):
        return kv.at[lax.rem(chip - k + chips, chips) * 2 + core]

    def relay_copy(k):
        block = arrived_block(k)
        return remote(block, block, rl_send.at[k], rl_recv.at[k], partner)

    def section_copy(k):
        return remote(sec.at[me], sec.at[me], sc_send, sc_recv, lax.rem(me + k, n))

    each(1, chips, lambda k: gather_copy(k).start())
    relay_copy(0).start()
    each(1, n, lambda k: section_copy(k).start())

    qrow = jnp.broadcast_to(qsec_ref[...], (8, count)).astype(F32)
    eye = (iota((count, count), 0) == iota((count, count), 1)).astype(BF16)
    qcol = dot(eye, qrow.astype(BF16), 1, 1)[:, 0:1]
    same = qcol == qrow[0:1, :]
    before = iota((count, count), 0) < iota((count, count), 1)
    after = iota((count, count), 1) < iota((count, count), 0)
    rank_row = jnp.sum(jnp.where(same & before, 1.0, 0.0), axis=0, keepdims=True)
    rank_col = jnp.sum(jnp.where(same & after, 1.0, 0.0), axis=1, keepdims=True)
    my_section = mine[0:1, 0:1].astype(F32)
    slot = (iota((SLOTS, count), 0) % READERS).astype(F32)
    pick = jnp.where((qrow[0:1, :] == my_section) & (rank_row == slot), 1.0, 0.0).astype(BF16)
    picked = dot(pick, sq_ref[...]).astype(BF16)
    low_rows = iota((SLOTS, HD), 0) < READERS
    qx = jnp.where(low_rows, picked[:, 0:HD].astype(F32), picked[:, HD:].astype(F32)).astype(BF16)
    q_flat = jnp.concatenate([q_ref[:, 0:HD], q_ref[:, HD : 2 * HD]], axis=0)

    def relay(k):
        gather_copy(k).wait_recv()
        relay_copy(k).start()

    each(1, chips, relay)
    others = sec.at[pl.ds(0, n - 1)]
    pltpu.make_async_copy(others, others, sc_recv).wait()
    each(0, chips, lambda k: relay_copy(k).wait_recv())

    sections = sec[...].reshape(n, HD).astype(F32).astype(BF16)

    block_spans = min(CHUNK // rows, n)
    width = block_spans * rows

    def scores_of(at):
        blocks = kv[pl.ds(at * block_spans, block_spans)].reshape(width, 2 * HD)
        keys = blocks[:, 0:HD]
        vals = blocks[:, HD : 2 * HD]
        s = dot(q_flat, keys, 1, 1) * scale
        x = dot(qx, keys, 1, 1) * scale
        spread = (
            iota((n, width), 0) == (iota((n, width), 1) // rows + at * block_spans)
        ).astype(BF16)
        token_section = dot(sections[:, 0:SLOTS], spread, 0, 0)
        mask = token_section == my_section
        return s, x, mask, vals

    def one(at, state):
        s, x, mask, vals = scores_of(at)
        top0, total0, acc0, xtop0, xtotal0 = state
        top = jnp.maximum(top0, jnp.max(s, axis=1, keepdims=True))
        shrink = jnp.exp(top0 - top)
        w = jnp.exp(s - top)
        total = total0 * shrink + jnp.sum(w, axis=1, keepdims=True)
        acc = acc0 * shrink + dot(w.astype(BF16), vals)
        xtop = jnp.maximum(
            xtop0, jnp.max(jnp.where(mask, x, F32(-1e30)), axis=1, keepdims=True)
        )
        xw = jnp.where(mask, jnp.exp(x - xtop), F32(0.0))
        xtotal = xtotal0 * jnp.exp(xtop0 - xtop) + jnp.sum(xw, axis=1, keepdims=True)
        return top, total, acc, xtop, xtotal

    state = (
        jnp.full((rows * HQ, 1), -1e30, F32),
        jnp.zeros((rows * HQ, 1), F32),
        jnp.zeros((rows * HQ, HD), F32),
        jnp.full((SLOTS, 1), -1e30, F32),
        jnp.zeros((SLOTS, 1), F32),
    )
    if n // block_spans == 1:
        state = one(0, state)
    else:
        state = lax.fori_loop(0, n // block_spans, one, state)
    top, total, acc, xtop, xtotal = state
    ctx = (acc / total).astype(BF16)
    own_x = dot(qx, kv[me][:, 0:HD], 1, 1) * scale
    own_w = jnp.exp(own_x - xtop).astype(BF16)
    p0 = dot(own_w, ctx[0:rows])
    p1 = dot(own_w, ctx[rows : 2 * rows])
    part[...] = (jnp.where(low_rows, p0, p1) / xtotal).astype(BF16)

    def part_copy(k):
        return remote(part, gath.at[me], pt_send, pt_recv, lax.rem(me + k, n))

    each(1, n, lambda k: part_copy(k).start())
    gath[me] = part[...]
    ctx_ref[:, 0:HD] = ctx[0:rows]
    ctx_ref[:, HD : 2 * HD] = ctx[rows : 2 * rows]

    wide = n * SLOTS
    tall = HQ * count
    owner = (iota((n, wide), 0) == iota((n, wide), 1) // SLOTS).astype(BF16)
    slot_section = dot(sections[:, 0:8], owner, 0, 0)[0:1, :]
    slot_rank = (iota((1, wide), 1) % READERS).astype(F32)
    slot_head = (iota((1, wide), 1) % SLOTS) // READERS
    hits = (qcol == slot_section) & (rank_col == slot_rank)
    choose = jnp.concatenate(
        [jnp.where(hits & (slot_head == h), 1.0, 0.0) for h in range(HQ)], axis=0
    ).astype(BF16)

    for w in weights:
        w.wait()
    seen = gath.at[pl.ds(0, n - 1)]
    pltpu.make_async_copy(seen, seen, pt_recv).wait()
    rows_in = gath[...].astype(F32).reshape(wide, HD).astype(BF16)
    pooled = dot(choose, rows_in).astype(BF16)
    pooled = jnp.concatenate([pooled[0:count], pooled[count:tall]], axis=1)
    embed = dot(pooled, ov[...])
    inv = lax.rsqrt(jnp.mean(embed * embed, axis=1, keepdims=True) + 1e-06)
    normed = (embed * inv * gain_ref[...].astype(F32)).astype(BF16)
    hidden = jax.nn.gelu(dot(normed, upv[...]), approximate=True).astype(BF16)

    span = out_ref.shape[1]
    y = dot(hidden, downv[...])
    for d in range(n):
        yb[d % 2, d // 2] = y[:, d * span : (d + 1) * span].astype(BF16)
    pair = remote(yb.at[1 - core], rb, pr_send, pr_recv, partner)
    pair.start()
    pair.wait_recv()

    def final_copy(k):
        to = lax.rem(chip + k, chips)
        return remote(
            sb.at[to], fb.at[k - 1], fn_send.at[k - 1], fn_recv.at[k - 1], to * 2 + core
        )

    def join(k):
        to = lax.rem(chip + k, chips)
        sb[to] = (yb[core, to].astype(F32) + rb[to].astype(F32)).astype(BF16)
        final_copy(k).start()

    each(1, chips, join)
    result = yb[core, chip].astype(F32) + rb[chip].astype(F32)
    if chips <= 16:
        for k in range(1, chips):
            final_copy(k).wait_recv()
            result = result + fb[k - 1].astype(F32)
    else:

        def take(k, value):
            final_copy(k).wait_recv()
            return value + fb[k - 1].astype(F32)

        result = lax.fori_loop(1, chips, take, result)
    out_ref[...] = result.astype(BF16)

    each(1, chips, lambda k: gather_copy(k).wait_send())
    each(0, chips, lambda k: relay_copy(k).wait_send())
    pltpu.make_async_copy(others, others, sc_send).wait()
    pltpu.make_async_copy(seen, seen, pt_send).wait()
    pair.wait_send()
    each(1, chips, lambda k: final_copy(k).wait_send())


def per_device(
    n,
    queries,
    keys,
    values,
    span_section,
    query_section,
    section_queries,
    out_proj,
    norm_gain,
    up_weight,
    down_weight,
):
    rows = queries.shape[0]
    count = section_queries.shape[0]
    features = out_proj.shape[1]
    span = features // n
    chips = n // 2
    dma = pltpu.SemaphoreType.DMA
    vmem = pl.BlockSpec(memory_space=pltpu.VMEM)
    smem = pl.BlockSpec(memory_space=pltpu.SMEM)
    anyw = pl.BlockSpec(memory_space=pl.ANY)
    return pl.pallas_call(
        functools.partial(kernel, n),
        out_shape=(
            jax.ShapeDtypeStruct(queries.shape, BF16),
            jax.ShapeDtypeStruct((count, span), BF16),
        ),
        in_specs=[vmem, anyw, anyw, smem, vmem, vmem, anyw, vmem, anyw, anyw],
        out_specs=(vmem, vmem),
        scratch_shapes=[
            pltpu.VMEM((n, rows, 2 * HD), BF16),
            pltpu.VMEM((n, 1, HD), jnp.int32),
            pltpu.VMEM((SLOTS, HD), BF16),
            pltpu.VMEM((n, SLOTS, HD), BF16),
            pltpu.VMEM(out_proj.shape, BF16),
            pltpu.VMEM(up_weight.shape, BF16),
            pltpu.VMEM(down_weight.shape, BF16),
            pltpu.VMEM((2, chips, count, span), BF16),
            pltpu.VMEM((chips, count, span), BF16),
            pltpu.VMEM((chips, count, span), BF16),
            pltpu.VMEM((chips - 1, count, span), BF16),
            dma((3,)),
            dma((2,)),
            dma((chips - 1,)),
            dma((chips - 1,)),
            dma((chips,)),
            dma((chips,)),
            dma,
            dma,
            dma,
            dma,
            dma,
            dma,
            dma((chips - 1,)),
            dma((chips - 1,)),
        ],
        compiler_params=pltpu.CompilerParams(
            collective_id=0, has_side_effects=True, vmem_limit_bytes=60 * 1024 * 1024
        ),
    )(
        queries,
        keys,
        values,
        span_section.reshape(1, 1),
        query_section.reshape(1, count),
        section_queries,
        out_proj,
        norm_gain.reshape(1, features),
        up_weight,
        down_weight,
    )


def solution(mesh):
    n = mesh.shape["ctx"]
    in_specs = (
        P(("groups", "ctx"), None),
        P(("groups", "ctx"), None),
        P(("groups", "ctx"), None),
        P(("groups", "ctx")),
        P("groups"),
        P("groups", None),
        P(),
        P(),
        P(None, "ctx"),
        P("ctx", None),
    )
    out_specs = (P(("groups", "ctx"), None), P("groups", "ctx"))
    return jax.shard_map(
        functools.partial(per_device, n),
        mesh=mesh,
        in_specs=in_specs,
        out_specs=out_specs,
        check_vma=False,
    )
```

time: 199 us -> 35.3 us (0.18)
  blocking collectives: 98.1 us -> 0 us
  waiting for transfers between devices: 60 us -> 0 us
  Pallas kernels: 0 us -> 29.6 us
  between operations: 15 us -> 1.29 us
  local copies, waits for them, and re-layouts: 10.6 us -> 4.04 us
  other arithmetic: 6.53 us -> 0 us
  matrix products: 6.43 us -> 0 us
    all_gather x5 -> x0, blocking collectives: 98.1 us -> none  [the longest x3 55.7 us: combined_all(): lax.all_gather(a.astype(kind), axis)]
    unnamed x2 -> x0, waiting for transfers between devices: 60 us -> none
    pallas_call x0 -> x1, Pallas kernels: none -> 29.6 us  [per_device(): pl.pallas_call(functools.partial(kernel, n), out_shape=(jax.ShapeDtypeStr...]
    dot_general x8 -> x0, matrix products: 6.43 us -> none  [the longest x1 3.86 us: per_device(): lax.dot_general(down_weight, hidden, (((0,), (1,)), ((), ())), preferred_...]
    add x32 -> x0, other arithmetic: 3.95 us -> none  [the longest x15 3.5 us: softmax_join(): first[2] * left[..., None] + second[2] * right[..., None]]
    exp x30 -> x0, local copies, waits for them, and re-layouts: 2.62 us -> none  [the longest x15 1.32 us: softmax_join(): right = jnp.exp(second[0] - top)]
  transfers between devices with their start and end apart: 1 -> 0, of which waited for: 1 -> 0; matrix products, arithmetic and copies ran while one was open for 0% -> 0% of each run, Pallas kernels for 0% -> 0%
where the time goes in v1:
time: 35.3 us; the launch traced here: 35 us
  Pallas kernels  29.6 us (84%)
  local copies, waits for them, and re-layouts  4.04 us (11%)
  between operations  1.29 us (4%)
    pallas_call x1, Pallas kernels, per_device(): pl.pallas_call(functools.partial(kernel, n), out_shape=(jax.ShapeDtypeStr...  29.6 us
    unnamed x2, local copies, waits for them, and re-layouts  2.72 us
    reshape x1, local copies, waits for them, and re-layouts, per_device(): norm_gain.reshape(1, features)  1.32 us

profile of v1, /device:TPU:0, one launch (start us, length us, event | category | flops | bytes accessed | tf_op | source)
XLA Modules:
  0.0 35.0 jit_solution(7428330921986725059)
XLA Ops:
  1.3 1.3 %reshape.15.gain_ref = bf16[1,4608]{1,0:T(2,128)(2,1)} reshape(bf16[4608]{0:T(1024)(128)(2,1)} %param.17) | data formatting | bytes 18432 | tf_op jit(solution)/shard_map/reshape | solution.py:366
  2.6 29.6 %shard_map.113 = (bf16[64,256]{1,0:T(8,128)(2,1)}, bf16[32,288]{1,0:T(8,128)(2,1)}) custom-call(bf16[64,256]{1,0:T(8,128)(2,1)} %q_ref.1, bf16[64,128]{1,0:T(8,128)(2,1)} %k_ref.1, bf16[64,128]{1,0:T(8,128)(2,1)} %v_ref.1, s32[1,1]{1,0:T(1,128)} %bitcast.2.span_ref, s32[1,32]{1,0:T(1,128)} %bitcast.3, bf16[32,256]{1,0:T(8,128)(2,1)} %sq_ref.1, ...), custom_call_target="tpu_custom_call" | custom-call | tf_op jit(solution)/shard_map/pallas_call | solution.py:320
  32.2 1.4 %copy.15 = bf16[64,256]{1,0:T(8,128)(2,1)} copy(bf16[64,256]{1,0:T(8,128)(2,1)} %get-tuple-element.4) | data formatting | bytes 65536
  33.6 1.3 %copy.16 = bf16[32,288]{1,0:T(8,128)(2,1)} copy(bf16[32,288]{1,0:T(8,128)(2,1)} %get-tuple-element.5) | data formatting | bytes 36864

commit v2 on v1

--- a/solution.py
+++ b/solution.py
@@ -11,6 +11,7 @@
 HQ = 2
 SPAN = 64
 READERS = 4
+MARK = 8
 CHUNK = 1024
 SLOTS = HQ * READERS
 
@@ -53,8 +54,13 @@
     down_ref,
     ctx_ref,
     out_ref,
+    qv,
+    qsecv,
+    sqv,
+    gainv,
+    ctxv,
+    outv,
     kv,
-    sec,
     part,
     gath,
     ov,
@@ -66,12 +72,12 @@
     fb,
     wsem,
     kvsem,
-    ag_send,
-    ag_recv,
-    rl_send,
-    rl_recv,
-    sc_send,
-    sc_recv,
+    z_send,
+    z_recv,
+    y_send,
+    y_recv,
+    c_send,
+    c_recv,
     pt_send,
     pt_recv,
     pr_send,
@@ -81,41 +87,60 @@
 ):
     scale = HD ** (-0.5)
     chips = n // 2
+    line = n // 4
     me = lax.axis_index("ctx")
     chip = me // 2
     core = me % 2
+    row = me // 4
+    side = chip % 2
     partner = me + 1 - 2 * core
+    across = me + 2 - 4 * side
     rows = q_ref.shape[0]
     tokens = n * rows
     count = qsec_ref.shape[1]
 
     own = kv.at[me]
-    kcopy = pltpu.make_async_copy(k_ref, own.at[:, 0:HD], kvsem.at[0])
-    vcopy = pltpu.make_async_copy(v_ref, own.at[:, HD : 2 * HD], kvsem.at[1])
-    kcopy.start()
-    vcopy.start()
+    kcopy = pltpu.make_async_copy(k_ref, own.at[0:rows, 0:HD], kvsem.at[0])
+    vcopy = pltpu.make_async_copy(v_ref, own.at[0:rows, HD : 2 * HD], kvsem.at[1])
+    small = [
+        pltpu.make_async_copy(src, dst, wsem.at[3 + i])
+        for i, (src, dst) in enumerate(
+            ((qsec_ref, qsecv), (sq_ref, sqv), (q_ref, qv), (gain_ref, gainv))
+        )
+    ]
     weights = [
         pltpu.make_async_copy(o_ref, ov, wsem.at[0]),
         pltpu.make_async_copy(up_ref, upv, wsem.at[1]),
         pltpu.make_async_copy(down_ref, downv, wsem.at[2]),
     ]
-    for w in weights:
-        w.start()
-
+    kcopy.start()
+    vcopy.start()
+
+    barrier = pltpu.get_barrier_semaphore()
+
+    def greet(to):
+        pl.semaphore_signal(barrier, inc=1, device_id={"ctx": to}, device_id_type=MESH)
+
+    greet(partner)
+    greet(across)
+
+    @pl.when(row > 0)
+    def _():
+        greet(me - 4)
+
+    @pl.when(row < line - 1)
+    def _():
+        greet(me + 4)
+
+    for c in small + weights:
+        c.start()
     mine = jnp.broadcast_to(span_ref[0, 0], (1, HD))
-    sec[me] = mine
-
-    barrier = pltpu.get_barrier_semaphore()
-
-    def greet(k):
-        pl.semaphore_signal(
-            barrier, inc=1, device_id={"ctx": lax.rem(me + k, n)}, device_id_type=MESH
-        )
-
-    each(1, n, greet)
-    pl.semaphore_wait(barrier, n - 1)
+    kv[me, rows : rows + MARK] = jnp.broadcast_to(span_ref[0, 0], (MARK, 2 * HD)).astype(
+        F32
+    ).astype(BF16)
     kcopy.wait()
     vcopy.wait()
+    pl.semaphore_wait(barrier, 2 + jnp.minimum(row, 1) + jnp.minimum(line - 1 - row, 1))
 
     def remote(src, dst, send, recv, to):
         return pltpu.make_async_remote_copy(
@@ -127,25 +152,36 @@
             device_id_type=MESH,
         )
 
-    def gather_copy(k):
-        to = lax.rem(chip + k, chips) * 2 + core
-        return remote(own, own, ag_send.at[k - 1], ag_recv.at[k - 1], to)
-
-    def arrived_block(k):
-        return kv.at[lax.rem(chip - k + chips, chips) * 2 + core]
-
-    def relay_copy(k):
-        block = arrived_block(k)
-        return remote(block, block, rl_send.at[k], rl_recv.at[k], partner)
-
-    def section_copy(k):
-        return remote(sec.at[me], sec.at[me], sc_send, sc_recv, lax.rem(me + k, n))
-
-    each(1, chips, lambda k: gather_copy(k).start())
-    relay_copy(0).start()
-    each(1, n, lambda k: section_copy(k).start())
-
-    qrow = jnp.broadcast_to(qsec_ref[...], (8, count)).astype(F32)
+    def line_copy(at, send, to):
+        block = kv.at[at * 4 + side * 2 + core]
+        return remote(block, block, z_send.at[send], z_recv.at[at], to)
+
+    def cross_copy(at, there):
+        block = kv.at[at * 4 + there * 2 + core]
+        return remote(block, block, y_send.at[at], y_recv.at[at], across)
+
+    def pair_copy(at, there, mate):
+        block = kv.at[at * 4 + there * 2 + mate]
+        sem = there * line + at
+        return remote(block, block, c_send.at[sem], c_recv.at[sem], partner)
+
+    def spread_row(at):
+        cross_copy(at, side).start()
+        pair_copy(at, side, core).start()
+
+    @pl.when(row < line - 1)
+    def _():
+        line_copy(row, row, me + 4).start()
+
+    @pl.when(row > 0)
+    def _():
+        line_copy(row, line, me - 4).start()
+
+    spread_row(row)
+
+    for c in small:
+        c.wait()
+    qrow = jnp.broadcast_to(qsecv[...], (8, count)).astype(F32)
     eye = (iota((count, count), 0) == iota((count, count), 1)).astype(BF16)
     qcol = dot(eye, qrow.astype(BF16), 1, 1)[:, 0:1]
     same = qcol == qrow[0:1, :]
@@ -156,29 +192,63 @@
     my_section = mine[0:1, 0:1].astype(F32)
     slot = (iota((SLOTS, count), 0) % READERS).astype(F32)
     pick = jnp.where((qrow[0:1, :] == my_section) & (rank_row == slot), 1.0, 0.0).astype(BF16)
-    picked = dot(pick, sq_ref[...]).astype(BF16)
+    picked = dot(pick, sqv[...]).astype(BF16)
     low_rows = iota((SLOTS, HD), 0) < READERS
     qx = jnp.where(low_rows, picked[:, 0:HD].astype(F32), picked[:, HD:].astype(F32)).astype(BF16)
-    q_flat = jnp.concatenate([q_ref[:, 0:HD], q_ref[:, HD : 2 * HD]], axis=0)
+    q_flat = jnp.concatenate([qv[:, 0:HD], qv[:, HD : 2 * HD]], axis=0)
+
+    def from_across(at):
+        cross_copy(at, 1 - side).wait_recv()
+        pair_copy(at, 1 - side, core).start()
 
     def relay(k):
-        gather_copy(k).wait_recv()
-        relay_copy(k).start()
-
-    each(1, chips, relay)
-    others = sec.at[pl.ds(0, n - 1)]
-    pltpu.make_async_copy(others, others, sc_recv).wait()
-    each(0, chips, lambda k: relay_copy(k).wait_recv())
-
-    sections = sec[...].reshape(n, HD).astype(F32).astype(BF16)
+        @pl.when(row >= k)
+        def _():
+            line_copy(row - k, row - k, partner).wait_recv()
+
+            @pl.when(row < line - 1)
+            def _():
+                line_copy(row - k, row - k, me + 4).start()
+
+            spread_row(row - k)
+
+        @pl.when(row + k < line)
+        def _():
+            line_copy(row + k, row + k, partner).wait_recv()
+
+            @pl.when(row > 0)
+            def _():
+                line_copy(row + k, row + k, me - 4).start()
+
+            spread_row(row + k)
+
+        behind(k - 1)
+
+    def behind(k):
+        @pl.when(row >= k)
+        def _():
+            from_across(row - k)
+
+        if not isinstance(k, int) or k > 0:
+
+            @pl.when((row + k < line) & (k > 0))
+            def _():
+                from_across(row + k)
+
+    each(1, line, relay)
+    behind(line - 1)
+    each(0, line, lambda k: pair_copy(k, 0, 1 - core).wait_recv())
+    each(0, line, lambda k: pair_copy(k, 1, 1 - core).wait_recv())
+
+    sections = kv[:, rows : rows + MARK, 0:HD].astype(F32)[:, 0, :].astype(BF16)
 
     block_spans = min(CHUNK // rows, n)
     width = block_spans * rows
 
     def scores_of(at):
-        blocks = kv[pl.ds(at * block_spans, block_spans)].reshape(width, 2 * HD)
-        keys = blocks[:, 0:HD]
-        vals = blocks[:, HD : 2 * HD]
+        span_at = pl.ds(at * block_spans, block_spans)
+        keys = kv[span_at, 0:rows, 0:HD].reshape(width, HD)
+        vals = kv[span_at, 0:rows, HD : 2 * HD].reshape(width, HD)
         s = dot(q_flat, keys, 1, 1) * scale
         x = dot(qx, keys, 1, 1) * scale
         spread = (
@@ -216,7 +286,7 @@
         state = lax.fori_loop(0, n // block_spans, one, state)
     top, total, acc, xtop, xtotal = state
     ctx = (acc / total).astype(BF16)
-    own_x = dot(qx, kv[me][:, 0:HD], 1, 1) * scale
+    own_x = dot(qx, kv[me, 0:rows, 0:HD], 1, 1) * scale
     own_w = jnp.exp(own_x - xtop).astype(BF16)
     p0 = dot(own_w, ctx[0:rows])
     p1 = dot(own_w, ctx[rows : 2 * rows])
@@ -227,8 +297,12 @@
 
     each(1, n, lambda k: part_copy(k).start())
     gath[me] = part[...]
-    ctx_ref[:, 0:HD] = ctx[0:rows]
-    ctx_ref[:, HD : 2 * HD] = ctx[rows : 2 * rows]
+    ctxv[:, 0:HD] = ctx[0:rows]
+    ctxv[:, HD : 2 * HD] = ctx[rows : 2 * rows]
+    ctx_out = pltpu.make_async_copy(ctxv, ctx_ref, kvsem.at[0])
+    ctx_out.start()
+    gain = gainv[...].astype(F32)
+    gain = jnp.concatenate([gain[i : i + 1] for i in range(gain.shape[0])], axis=1)
 
     wide = n * SLOTS
     tall = HQ * count
@@ -250,7 +324,7 @@
     pooled = jnp.concatenate([pooled[0:count], pooled[count:tall]], axis=1)
     embed = dot(pooled, ov[...])
     inv = lax.rsqrt(jnp.mean(embed * embed, axis=1, keepdims=True) + 1e-06)
-    normed = (embed * inv * gain_ref[...].astype(F32)).astype(BF16)
+    normed = (embed * inv * gain).astype(BF16)
     hidden = jax.nn.gelu(dot(normed, upv[...]), approximate=True).astype(BF16)
 
     span = out_ref.shape[1]
@@ -285,14 +359,51 @@
             return value + fb[k - 1].astype(F32)
 
         result = lax.fori_loop(1, chips, take, result)
-    out_ref[...] = result.astype(BF16)
-
-    each(1, chips, lambda k: gather_copy(k).wait_send())
-    each(0, chips, lambda k: relay_copy(k).wait_send())
-    pltpu.make_async_copy(others, others, sc_send).wait()
+    outv[...] = result.astype(BF16)
+    final_out = pltpu.make_async_copy(outv, out_ref, kvsem.at[1])
+    final_out.start()
+
+    @pl.when(row < line - 1)
+    def _():
+        line_copy(row, row, partner).wait_send()
+
+    @pl.when(row > 0)
+    def _():
+        line_copy(row, line, partner).wait_send()
+
+    def sent(at):
+        @pl.when(((at < row) & (row < line - 1)) | ((at > row) & (row > 0)))
+        def _():
+            line_copy(at, at, partner).wait_send()
+
+        cross_copy(at, side).wait_send()
+        pair_copy(at, 0, core).wait_send()
+        pair_copy(at, 1, core).wait_send()
+
+    each(0, line, sent)
     pltpu.make_async_copy(seen, seen, pt_send).wait()
     pair.wait_send()
     each(1, chips, lambda k: final_copy(k).wait_send())
+    ctx_out.wait()
+    final_out.wait()
+
+
+def hand_over(a_ref, b_ref, c_ref, d_ref, av, bv, sems):
+    into = (
+        pltpu.make_async_copy(a_ref, av, sems.at[0]),
+        pltpu.make_async_copy(b_ref, bv, sems.at[1]),
+    )
+    out = (
+        pltpu.make_async_copy(av, c_ref, sems.at[2]),
+        pltpu.make_async_copy(bv, d_ref, sems.at[3]),
+    )
+    for c in into:
+        c.start()
+    for c, o in zip(into, out):
+        c.wait()
+        o.start()
+    for o in out:
+        o.wait()
 
 
 def per_device(
@@ -313,21 +424,27 @@
     features = out_proj.shape[1]
     span = features // n
     chips = n // 2
+    line = n // 4
     dma = pltpu.SemaphoreType.DMA
     vmem = pl.BlockSpec(memory_space=pltpu.VMEM)
     smem = pl.BlockSpec(memory_space=pltpu.SMEM)
     anyw = pl.BlockSpec(memory_space=pl.ANY)
-    return pl.pallas_call(
+    result = pl.pallas_call(
         functools.partial(kernel, n),
         out_shape=(
             jax.ShapeDtypeStruct(queries.shape, BF16),
             jax.ShapeDtypeStruct((count, span), BF16),
         ),
-        in_specs=[vmem, anyw, anyw, smem, vmem, vmem, anyw, vmem, anyw, anyw],
-        out_specs=(vmem, vmem),
+        in_specs=[anyw, anyw, anyw, smem, anyw, anyw, anyw, anyw, anyw, anyw],
+        out_specs=(anyw, anyw),
         scratch_shapes=[
-            pltpu.VMEM((n, rows, 2 * HD), BF16),
-            pltpu.VMEM((n, 1, HD), jnp.int32),
+            pltpu.VMEM(queries.shape, BF16),
+            pltpu.VMEM((1, count), jnp.int32),
+            pltpu.VMEM(section_queries.shape, BF16),
+            pltpu.VMEM((features // HD, HD), BF16),
+            pltpu.VMEM(queries.shape, BF16),
+            pltpu.VMEM((count, span), BF16),
+            pltpu.VMEM((n, rows + MARK, 2 * HD), BF16),
             pltpu.VMEM((SLOTS, HD), BF16),
             pltpu.VMEM((n, SLOTS, HD), BF16),
             pltpu.VMEM(out_proj.shape, BF16),
@@ -337,14 +454,14 @@
             pltpu.VMEM((chips, count, span), BF16),
             pltpu.VMEM((chips, count, span), BF16),
             pltpu.VMEM((chips - 1, count, span), BF16),
-            dma((3,)),
+            dma((7,)),
             dma((2,)),
-            dma((chips - 1,)),
-            dma((chips - 1,)),
+            dma((line + 1,)),
+            dma((line,)),
+            dma((line,)),
+            dma((line,)),
             dma((chips,)),
             dma((chips,)),
-            dma,
-            dma,
             dma,
             dma,
             dma,
@@ -363,10 +480,24 @@
         query_section.reshape(1, count),
         section_queries,
         out_proj,
-        norm_gain.reshape(1, features),
+        norm_gain.reshape(features // HD, HD),
         up_weight,
         down_weight,
     )
+    return pl.pallas_call(
+        hand_over,
+        out_shape=(
+            jax.ShapeDtypeStruct(queries.shape, BF16),
+            jax.ShapeDtypeStruct((count, span), BF16),
+        ),
+        in_specs=[anyw, anyw],
+        out_specs=(anyw, anyw),
+        scratch_shapes=[
+            pltpu.VMEM(queries.shape, BF16),
+            pltpu.VMEM((count, span), BF16),
+            dma((4,)),
+        ],
+    )(*result)
 
 
 def solution(mesh):

time: 35.3 us -> 33.6 us (0.952)
  local copies, waits for them, and re-layouts: 4.04 us -> 0 us
  Pallas kernels: 29.6 us -> 32 us
    unnamed x2 -> x0, local copies, waits for them, and re-layouts: 2.72 us -> none
    pallas_call x0 -> x1, Pallas kernels: none -> 1.41 us  [per_device(): pl.pallas_call(hand_over, out_shape=(jax.ShapeDtypeStruct(queries.shape,...]
    reshape x1 -> x0, local copies, waits for them, and re-layouts: 1.32 us -> none  [per_device(): norm_gain.reshape(1, features)]
    pallas_call x1, Pallas kernels: 29.6 us -> 30.6 us  [per_device(): pl.pallas_call(functools.partial(kernel, n), out_shape=(jax.ShapeDtypeStr...]
where the time goes in v2:
time: 33.6 us; the launch traced here: 33.3 us
  Pallas kernels  32 us (95%)
  between operations  1.29 us (4%)
    pallas_call x1, Pallas kernels, per_device(): pl.pallas_call(functools.partial(kernel, n), out_shape=(jax.ShapeDtypeStr...  30.6 us
    pallas_call x1, Pallas kernels, per_device(): pl.pallas_call(hand_over, out_shape=(jax.ShapeDtypeStruct(queries.shape,...  1.41 us

profile of v2, /device:TPU:0, one launch (start us, length us, event | category | flops | bytes accessed | tf_op | source)
XLA Modules:
  0.0 33.3 jit_solution(15832951668279245223)
XLA Ops:
  1.3 30.6 %shard_map.113 = (bf16[64,256]{1,0:T(8,128)(2,1)}, bf16[32,288]{1,0:T(8,128)(2,1)}) custom-call(bf16[64,256]{1,0:T(8,128)(2,1)} %q_ref.1, bf16[64,128]{1,0:T(8,128)(2,1)} %k_ref.1, bf16[64,128]{1,0:T(8,128)(2,1)} %v_ref.1, s32[1,1]{1,0:T(1,128)} %bitcast.3.span_ref, s32[1,32]{1,0:T(1,128)} %bitcast.5, bf16[32,256]{1,0:T(8,128)(2,1)} %sq_ref.1, ...), custom_call_target="tpu_custom_call" | custom-call | tf_op jit(solution)/shard_map/pallas_call | solution.py:432
  31.9 1.4 %shard_map.114 = (bf16[64,256]{1,0:T(8,128)(2,1)}, bf16[32,288]{1,0:T(8,128)(2,1)}) custom-call(bf16[64,256]{1,0:T(8,128)(2,1)} %get-tuple-element.4.a_ref, bf16[32,288]{1,0:T(8,128)(2,1)} %get-tuple-element.5.b_ref), custom_call_target="tpu_custom_call" | custom-call | tf_op jit(solution)/shard_map/pallas_call | solution.py:487
